TPU v7x, 32 devices: a whole 2x2x4 slice. The times are simulated.
32 devices in a mesh: groups: 2 (over y), seq: 4 (over z), req: 2 (over x), head: 2 (over core).
Axes of the slice: x: 2, y: 2, z: 4, core: 2. Of those that a mesh axis runs over, the one named last changes fastest.
Arguments:
- cache: bfloat16 [8, 6144, 576], P(('groups', 'req'), 'seq'), parts along dimension 0, may hold values from -4 to 4
- index_key: bfloat16 [8, 6144, 128], P(('groups', 'req'), 'seq'), parts along dimension 0, may hold values from -4 to 4
- index_scale: float32 [8, 6144], P(('groups', 'req'), 'seq'), parts along dimension 0, may hold values from 1.5 to 12
- lengths: int32 [8], P(('groups', 'req')), parts along dimension 0, may hold values from 4608 to 6143, as said below
- owners: int32 [8], P(('groups', 'req')), parts along dimension 0, may hold values from 0 to 3, as said below
- selected: int32 [2, 8, 2048], P(None, ('groups', 'req')), parts along dimension 1, may hold values from 0 to 6143, as said below
- query: bfloat16 [2, 16, 128, 576], P(None, ('groups', 'seq', 'req'), 'head'), parts along dimension 1, may hold values from -41 to 41
- index_query: bfloat16 [2, 16, 64, 128], P(None, ('groups', 'seq', 'req')), parts along dimension 1, may hold values from -0.5 to 0.5
- index_weight: bfloat16 [2, 16, 64], P(None, ('groups', 'seq', 'req')), parts along dimension 1, may hold values from -0.75 to 0.75
Outputs:
- index_scores: float32 [2, 8, 6144], P(None, ('groups', 'req'), 'seq'), parts along dimension 1
- threshold: float32 [2, 8], P(None, ('groups', 'req')), parts along dimension 1
- attended: bfloat16 [2, 16, 128, 512], P(None, ('groups', 'seq', 'req'), 'head'), parts along dimension 1
There are 2 independent parts, one for each index of `groups`. A program takes and returns all parts, laid end to end along the dimension named above; each array names one. Nothing has to cross between parts.
Inputs may be any that keep to these rules, and one draw needn't show every extreme that they name: `lengths`: some request of each group has length 6143. The 2 requests i * 2 to (i + 1) * 2 - 1 have distinct owners. selected[t, r] holds 2048 distinct positions below lengths[r] + t; at most 768 of them lie in one block of positions k * 1536 to (k + 1) * 1536 - 1, and in every list some block holds exactly 768.
All inputs are finite; a program needn't handle non-finite values.
Results may differ from a plain program's by a relative error of at most 0.007.
Values may be sent and summed in bfloat16 or wider, within the bound.
No kernel may reach another device: no remote copies, remote signals or barrier semaphores. Data moves between devices by JAX's collectives and lax.ppermute only.
A program may use at most 64 MiB of HBM per device.

v0:
```python
import jax
import jax.numpy as jnp
from jax import lax
from jax.sharding import PartitionSpec as P

ROPE = 64


score_scale = 192.0 ** (-0.5)
masked_value = -1e30


def combined_all(x, axis, join):
    gathered = lax.all_gather(x.astype(jnp.bfloat16), axis)

    def take(source):
        return lax.dynamic_index_in_dim(gathered, source, 0, False).astype(x.dtype)

    return lax.fori_loop(
        1, lax.axis_size(axis), lambda source, state: join(state, take(source)), take(0)
    )


def top_values(earlier, later):
    keep_count = earlier.shape[-1]
    return lax.top_k(jnp.concatenate([earlier, later], axis=-1), keep_count)[0]


def shards(
    cache, index_key, index_scale, lengths, owners, selected, query, index_query, index_weight
):
    seq_count = lax.axis_size("seq")
    seq_rank = lax.axis_index("seq")
    local_requests = cache.shape[0]
    shard_rows = cache.shape[1]
    row_width = cache.shape[2]
    step_count = selected.shape[0]
    select_count = selected.shape[2]
    latent_width = row_width - ROPE
    capacity = shard_rows // 2
    step_ids = jnp.arange(step_count, dtype=jnp.int32)
    seq_ids = jnp.arange(seq_count, dtype=jnp.int32)
    request_ids = jnp.arange(local_requests, dtype=jnp.int32)
    owner_table = owners[:, None] == seq_ids[None, :]
    picker = owner_table.astype(jnp.bfloat16)
    dest_request = jnp.sum(owner_table.astype(jnp.int32) * request_ids[:, None], axis=0)
    owned_here = owners == seq_rank
    holds_request = jnp.any(owned_here)
    heads_query, heads_weight = (
        lax.all_gather(index_query, "seq", axis=1, tiled=True),
        lax.all_gather(index_weight, "seq", axis=1, tiled=True),
    )
    owner_query = jnp.einsum(
        "jo,tohd->tjhd", picker, heads_query, preferred_element_type=jnp.float32
    ).astype(jnp.bfloat16)
    owner_weight = jnp.einsum(
        "jo,toh->tjh", picker, heads_weight, preferred_element_type=jnp.float32
    )
    raw_dots = jnp.einsum(
        "tjhd,jpd->tjhp", owner_query, index_key, preferred_element_type=jnp.float32
    )
    scores = jnp.sum(jax.nn.relu(raw_dots) * owner_weight[..., None], axis=2) * index_scale[None]
    positions = seq_rank * shard_rows + jnp.arange(shard_rows, dtype=jnp.int32)
    in_length = positions[None, None, :] < lengths[None, :, None] + step_ids[:, None, None]
    index_scores = jnp.where(in_length, scores, 0.0)
    candidates = jnp.where(in_length, scores, masked_value)
    candidates = jnp.pad(
        candidates, ((0, 0), (0, 0), (0, select_count - shard_rows)), constant_values=masked_value
    )
    ranked = combined_all(candidates, "seq", top_values)
    threshold = ranked[..., select_count - 1]
    owning = selected // shard_rows == seq_rank
    placing = jnp.cumsum(owning.astype(jnp.int32), axis=2) - 1
    counts = jnp.sum(owning.astype(jnp.int32), axis=2)
    target = jnp.where(owning, placing, capacity)
    local_position = selected - seq_rank * shard_rows
    step_grid = jnp.broadcast_to(step_ids[:, None, None], selected.shape)
    request_grid = jnp.broadcast_to(request_ids[None, :, None], selected.shape)
    slot_position = jnp.zeros((step_count, local_requests, capacity + 1), jnp.int32)
    slot_position = slot_position.at[step_grid, request_grid, target].set(local_position)[
        :, :, :capacity
    ]
    flat_cache = cache.reshape(local_requests * shard_rows, row_width)
    slot_ids = jnp.arange(capacity, dtype=jnp.int32)
    all_queries = lax.all_gather(query, "seq", axis=1, tiled=True)
    request_query = jnp.einsum(
        "jo,tohd->tjhd", picker, all_queries, preferred_element_type=jnp.float32
    ).astype(jnp.bfloat16)
    local_rows = jnp.take(
        flat_cache, request_ids[None, :, None] * shard_rows + slot_position, axis=0
    )
    usable = (slot_ids[None, None, :] < counts[:, :, None])[:, :, None, :]
    logits = (
        jnp.einsum("tjhd,tjcd->tjhc", request_query, local_rows, preferred_element_type=jnp.float32)
        * score_scale
    )
    logits = jnp.where(usable, logits, masked_value)
    row_peak = jnp.max(logits, axis=3)
    weights = jnp.where(usable, jnp.exp(logits - row_peak[..., None]), 0.0)
    row_total = jnp.sum(weights, axis=3)
    mixture = jnp.einsum(
        "tjhc,tjcd->tjhd",
        weights.astype(jnp.bfloat16),
        local_rows,
        preferred_element_type=jnp.float32,
    )[..., :latent_width]
    outbound = (
        jnp.take(mixture, dest_request, axis=1),
        jnp.take(row_peak, dest_request, axis=1),
        jnp.take(row_total, dest_request, axis=1),
    )
    got_mixture, got_peak, got_total = (
        lax.all_to_all(outbound[0], "seq", split_axis=1, concat_axis=1, tiled=True),
        lax.all_to_all(outbound[1], "seq", split_axis=1, concat_axis=1, tiled=True),
        lax.all_to_all(outbound[2], "seq", split_axis=1, concat_axis=1, tiled=True),
    )
    highest = jnp.max(got_peak, axis=1, keepdims=True)
    rescale = jnp.exp(got_peak - highest)
    merged = jnp.sum(got_mixture * rescale[..., None], axis=1)
    result = merged / jnp.sum(got_total * rescale, axis=1)[..., None]
    attended = jnp.where(holds_request, result, 0.0).astype(jnp.bfloat16)[:, None]
    return (index_scores, threshold, attended)


def solution(mesh):
    placed = (
        P(("groups", "req"), "seq", None),
        P(("groups", "req"), "seq", None),
        P(("groups", "req"), "seq"),
        P(("groups", "req")),
        P(("groups", "req")),
        P(None, ("groups", "req"), None),
        P(None, ("groups", "seq", "req"), "head", None),
        P(None, ("groups", "seq", "req"), None, None),
        P(None, ("groups", "seq", "req"), None),
    )
    return jax.shard_map(
        shards,
        mesh=mesh,
        in_specs=placed,
        out_specs=(
            P(None, ("groups", "req"), "seq"),
            P(None, ("groups", "req")),
            P(None, ("groups", "seq", "req"), "head", None),
        ),
        check_vma=False,
    )
```

profile of v0, /device:TPU:0, one launch (start us, length us, event | category | flops | bytes accessed | tf_op | source)
XLA Modules:
  0.0 209.9 jit_solution(12546323164927925906)
XLA Ops:
  0.7 0.8 select_reduce_fusion
  1.5 1.0 convert_reduce_fusion
  2.5 1.2 reduce-window.6
  3.7 0.2 slice_reduce_fusion
  3.9 0.4 reduce-window.9
  4.5 0.8 multiply_reduce_fusion.1
  5.3 0.8 and_reduce_fusion
  6.2 30.5 %scatter_custom_fusion = s32[3076]{0:T(1024)S(1)} fusion(s32[8192]{0:T(1024)S(1)} %bitcast.77, s32[8192]{0:T(1024)S(1)} %bitcast.78, s32[]{:T(128)} %constant.120.clone.1), kind=kCustom, calls=%fused_computation.56 | custom fusion | bytes 12308
  36.7 0.1 compare_and_fusion
  36.9 5.9 %copy.42 = bf16[2,1536,576]{2,1,0:T(8,128)(2,1)} copy(bf16[2,1536,576]{1,2,0:T(8,128)(2,1)} %param.13) | data formatting | bytes 7077888 | tf_op args[0]
  42.8 16.4 %gather_fusion = bf16[3072,576]{1,0:T(8,128)(2,1)} fusion(bf16[3072,576]{1,0:T(8,128)(2,1)} %bitcast.72, s32[3072]{0:T(1024)S(1)} %broadcast_clamp_fusion), kind=kCustom, calls=%fused_computation.2 | custom fusion | bytes 7090176 | tf_op jit(solution)/shard_map/jit(_take)/gather | solution.py:89
  59.2 6.2 %copy.43 = bf16[2,2,768,576]{2,3,1,0:T(8,128)(2,1)} copy(bf16[2,2,768,576]{3,2,1,0:T(8,128)(2,1)} %bitcast.73) | data formatting | bytes 7077888 | tf_op jit(solution)/shard_map/jit(_take)/gather | solution.py:89
  65.5 19.7 %all_gather.19 = bf16[2,4,64,576]{3,2,0,1:T(8,128)(2,1)S(1)} all-gather(bf16[2,1,64,576]{3,2,0,1:T(8,128)(2,1)S(1)} %bitcast.75), channel_id=1, replica_groups=mesh['groups'=2,'seq'=4,'req'=2,'head'=2] {'seq'}, dimensions={1}, use_global_device_ids=true | all-gather | bytes 737280 | tf_op jit(solution)/shard_map/all_gather | solution.py:85
  85.2 0.6 fusion.6
  85.8 2.3 %broadcast_select_fusion = bf16[2,2,768,576]{2,3,1,0:T(8,128)(2,1)S(1)} fusion(bf16[2,2,768,576]{2,3,1,0:T(8,128)(2,1)} %copy.43, pred[2,2,768]{2,1,0:T(4,128)(4,1)S(1)} %get-tuple-element.111), kind=kLoop, calls=%fused_computation.7 | loop fusion | flops 1769472 | bytes 7080960 | tf_op jit(solution)/shard_map/jit(_take)/select_n | solution.py:89
  88.2 1.7 copy-done.1
  89.9 0.9 fusion.36
  90.8 0.3 fusion.10
  91.2 0.6 gather_fusion.3
  91.7 0.6 gather_fusion.2
  92.4 0.7 reshape.174
  93.1 3.8 %all-to-all-start.1 = ((f32[4,1,128]{2,1,0:T(1,128)}), f32[4,1,128]{2,1,0:T(1,128)S(1)}, u32[]{:S(2)}, u32[]{:S(2)}) async-start(f32[4,1,128]{2,1,0:T(1,128)} %reshape.174), calls=%async_computation.1 | async-start | bytes 4096 | tf_op jit(solution)/shard_map/all_to_all | solution.py:114
  96.8 3.0 %fusion = f32[2,2,64,512]{3,2,1,0:T(8,128)S(1)} fusion(bf16[2,2,768,576]{2,3,1,0:T(8,128)(2,1)} %copy-done.1, f32[2,2,64,768]{3,2,1,0:T(8,128)S(1)} %get-tuple-element.119, f32[2,2,64]{2,1,0:T(2,128)S(1)} %get-tuple-element.118, pred[2,2,768]{2,1,0:T(4,128)(4,1)S(1)} %iota_compare_fusion), kind=kOutput, calls=%fused_computation.8 | convolution fusion | flops 201916416 | bytes 4460544 | tf_op jit(solution)/shard_map/tjhc,tjcd->tjhd/dot_general | solution.py:101
  99.9 13.9 %all_gather.15 = bf16[2,4,64,128]{3,2,0,1:T(8,128)(2,1)S(1)} all-gather(bf16[2,1,64,128]{3,2,0,1:T(8,128)(2,1)S(1)} %bitcast.76), channel_id=1, replica_groups=mesh['groups'=2,'seq'=4,'req'=2,'head'=2] {'seq'}, dimensions={1}, use_global_device_ids=true | all-gather | bytes 163840 | tf_op jit(solution)/shard_map/all_gather | solution.py:50
  113.8 0.3 fusion.7
  114.1 10.9 %all_gather.16 = bf16[2,4,64]{2,0,1:T(2,128)(2,1)S(1)} all-gather(bf16[2,1,64]{2,0,1:T(2,128)(2,1)S(1)} %copy-done.5), channel_id=1, replica_groups=mesh['groups'=2,'seq'=4,'req'=2,'head'=2] {'seq'}, dimensions={1}, use_global_device_ids=true | all-gather | bytes 1280 | tf_op jit(solution)/shard_map/all_gather | solution.py:51
  124.9 0.2 convolution_bitcast_fusion
  125.2 0.4 fusion.4
  125.6 0.1 fusion.23
  125.7 13.1 %all-gather = bf16[8,2,2048]{2,1,0:T(2,128)(2,1)S(1)} all-gather(bf16[2,2,2048]{2,1,0:T(2,128)(2,1)S(1)} %pad.5.clone), channel_id=2, replica_groups=mesh['groups'=2,'seq'=4,'req'=2,'head'=2] {'seq'}, dimensions={0}, use_global_device_ids=true | all-gather | bytes 81920 | tf_op jit(solution)/shard_map/all_gather | solution.py:14
  138.9 0.6 gather_fusion.1
  139.5 1.2 select_bitcast_fusion
  140.7 0.7 reshape.176
  141.4 3.2 %all-to-all-start.2 = ((f32[4,1,128]{2,1,0:T(1,128)}), f32[4,1,128]{2,1,0:T(1,128)S(1)}, u32[]{:S(2)}, u32[]{:S(2)}) async-start(f32[4,1,128]{2,1,0:T(1,128)} %reshape.176), calls=%async_computation.2 | async-start | bytes 4096 | tf_op jit(solution)/shard_map/all_to_all | solution.py:115
  144.6 0.7 compare_reduce_fusion
  145.3 0.6 copy.47
  146.0 4.1 %all-to-all-done.2 = f32[4,1,128]{2,1,0:T(1,128)S(1)} async-done(((f32[4,1,128]{2,1,0:T(1,128)}), f32[4,1,128]{2,1,0:T(1,128)S(1)}, u32[]{:S(2)}, u32[]{:S(2)}) %all-to-all-start.2) | async-done | bytes 2080 | tf_op jit(solution)/shard_map/all_to_all | solution.py:115
  150.1 5.6 %all-to-all-start = ((f32[2,4,64,512]{3,2,0,1:T(8,128)}), f32[2,4,64,512]{3,2,0,1:T(8,128)S(1)}, u32[]{:S(2)}, u32[]{:S(2)}) async-start(f32[2,4,64,512]{3,2,0,1:T(8,128)} %select_bitcast_fusion), calls=%async_computation | async-start | bytes 2097152 | tf_op jit(solution)/shard_map/all_to_all | solution.py:113
  155.7 49.8 %while.15 = (s32[]{:T(128)}, f32[2,2,2048]{2,1,0:T(2,128)S(1)}, bf16[4,2,2,2048]{3,2,1,0:T(2,128)(2,1)S(1)}, s32[]{:T(128)}, s32[]{:T(128)}, /*index=5*/s32[]{:T(128)}) while((s32[]{:T(128)}, f32[2,2,2048]{2,1,0:T(2,128)S(1)}, bf16[4,2,2,2048]{3,2,1,0:T(2,128)(2,1)S(1)}, s32[]{:T(128)}, s32[]{:T(128)}, /*index=5*/s32[]{:T(128)}) %tuple.53), condition=%wide.region_3.4_spmd, body=%wide.region_1.3_spmd.sunk | while | flops 253957 | bytes 573555 | solution.py:19
  155.8 16.5 %top_k.11 = (f32[2,2,4096]{2,1,0:T(2,128)S(1)}, s32[2,2,4096]{2,1,0:T(2,128)}) sort(f32[2,2,4096]{2,1,0:T(2,128)S(1)} %pad_maximum_fusion.2, s32[2,2,4096]{2,1,0:T(2,128)S(1)} %iota.45), dimensions={2}, to_apply=%region_2.2 | sort | flops 229376 | bytes 262144 | tf_op jit(solution)/shard_map/while/body/eval_jaxpr/top_k | solution.py:26
  172.4 16.5 %top_k.11 = (f32[2,2,4096]{2,1,0:T(2,128)S(1)}, s32[2,2,4096]{2,1,0:T(2,128)}) sort(f32[2,2,4096]{2,1,0:T(2,128)S(1)} %pad_maximum_fusion.2, s32[2,2,4096]{2,1,0:T(2,128)S(1)} %iota.45), dimensions={2}, to_apply=%region_2.2 | sort | flops 229376 | bytes 262144 | tf_op jit(solution)/shard_map/while/body/eval_jaxpr/top_k | solution.py:26
  189.0 16.5 %top_k.11 = (f32[2,2,4096]{2,1,0:T(2,128)S(1)}, s32[2,2,4096]{2,1,0:T(2,128)}) sort(f32[2,2,4096]{2,1,0:T(2,128)S(1)} %pad_maximum_fusion.2, s32[2,2,4096]{2,1,0:T(2,128)S(1)} %iota.45), dimensions={2}, to_apply=%region_2.2 | sort | flops 229376 | bytes 262144 | tf_op jit(solution)/shard_map/while/body/eval_jaxpr/top_k | solution.py:26
  205.5 0.7 slice_reduce_fusion.1
  206.2 0.5 broadcast.224
  206.7 0.7 reduce.8
  207.5 0.7 reduce.9
  208.3 0.1 multiply_reduce_fusion
  208.4 1.4 fusion.18
  (62 shorter events, 1.1 us)
Async XLA Ops:
  0.6 124.6 %copy-start = (bf16[2,1536,128]{2,1,0:T(8,128)(2,1)S(1)}, bf16[2,1536,128]{2,1,0:T(8,128)(2,1)}, u32[]{:S(2)}) copy-start(bf16[2,1536,128]{2,1,0:T(8,128)(2,1)} %param.14) | copy-start | bytes 2359300
  59.2 6.3 %copy-start.2 = (bf16[2,1,64,576]{3,2,1,0:T(8,128)(2,1)S(1)}, bf16[2,1,64,576]{3,2,1,0:T(8,128)(2,1)}, u32[]{:S(2)}) copy-start(bf16[2,1,64,576]{3,2,1,0:T(8,128)(2,1)} %param.19) | copy-start | bytes 442372
  59.2 26.0 %copy-start.7 = (s32[2]{0:T(128)S(1)}, s32[2]{0:T(128)}, u32[]{:S(2)}) copy-start(s32[2]{0:T(128)} %param.17) | copy-start | bytes 28
  88.2 1.8 copy-start.1
  90.8 9.1 %copy-start.3 = (bf16[2,1,64,128]{3,2,1,0:T(8,128)(2,1)S(1)}, bf16[2,1,64,128]{3,2,1,0:T(8,128)(2,1)}, u32[]{:S(2)}) copy-start(bf16[2,1,64,128]{3,2,1,0:T(8,128)(2,1)} %param.20) | copy-start | bytes 98308
  90.8 23.3 %copy-start.5 = (bf16[2,1,64]{2,0,1:T(2,128)(2,1)S(1)}, bf16[2,1,64]{2,0,1:T(2,128)(2,1)}, u32[]{:S(2)}) copy-start(bf16[2,1,64]{2,0,1:T(2,128)(2,1)} %param.21) | copy-start | bytes 772
  90.8 34.3 %copy-start.6 = (s32[2]{0:T(128)S(1)}, s32[2]{0:T(128)}, u32[]{:S(2)}) copy-start(s32[2]{0:T(128)} %param.16) | copy-start | bytes 28
  91.1 34.5 %copy-start.4 = (f32[2,1536]{1,0:T(2,128)S(1)}, f32[2,1536]{1,0:T(2,128)}, u32[]{:S(2)}) copy-start(f32[2,1536]{1,0:T(2,128)} %param.15) | copy-start | bytes 36868
  93.1 48.3 %all-to-all-start.1 = ((f32[4,1,128]{2,1,0:T(1,128)}), f32[4,1,128]{2,1,0:T(1,128)S(1)}, u32[]{:S(2)}, u32[]{:S(2)}) async-start(f32[4,1,128]{2,1,0:T(1,128)} %reshape.174), calls=%async_computation.1 | async-start | bytes 4096 | tf_op jit(solution)/shard_map/all_to_all | solution.py:114
  141.4 8.7 %all-to-all-start.2 = ((f32[4,1,128]{2,1,0:T(1,128)}), f32[4,1,128]{2,1,0:T(1,128)S(1)}, u32[]{:S(2)}, u32[]{:S(2)}) async-start(f32[4,1,128]{2,1,0:T(1,128)} %reshape.176), calls=%async_computation.2 | async-start | bytes 4096 | tf_op jit(solution)/shard_map/all_to_all | solution.py:115
  150.1 58.2 %all-to-all-start = ((f32[2,4,64,512]{3,2,0,1:T(8,128)}), f32[2,4,64,512]{3,2,0,1:T(8,128)S(1)}, u32[]{:S(2)}, u32[]{:S(2)}) async-start(f32[2,4,64,512]{3,2,0,1:T(8,128)} %select_bitcast_fusion), calls=%async_computation | async-start | bytes 2097152 | tf_op jit(solution)/shard_map/all_to_all | solution.py:113
where the time goes:
time: 211 us; the launch traced here: 210 us
  local copies, waits for them, and re-layouts  66.4 us (31%)
  other arithmetic  62.7 us (30%)
  blocking collectives  57.6 us (27%)
  starting transfers between devices  12.7 us (6%)
  matrix products  5.33 us (3%)
  waiting for transfers between devices  4.14 us (2%)
    top_k x3, other arithmetic, top_values(): return lax.top_k(jnp.concatenate([earlier, later], axis=-1), keep_count)[0]  49.5 us
    unnamed x26, local copies, waits for them, and re-layouts  40.3 us
    gather x2, local copies, waits for them, and re-layouts, shards(): jnp.take(flat_cache, request_ids[None, :, None] * shard_rows + slot_posit...  22.6 us
    all_gather x1, blocking collectives, shards(): all_queries = lax.all_gather(query, 'seq', axis=1, tiled=True)  19.7 us
    all_gather x1, blocking collectives, shards(): lax.all_gather(index_query, 'seq', axis=1, tiled=True)  13.9 us
    all_gather x1, blocking collectives, combined_all(): gathered = lax.all_gather(x.astype(jnp.bfloat16), axis)  13.1 us
    all_gather x1, blocking collectives, shards(): lax.all_gather(index_weight, 'seq', axis=1, tiled=True)  10.9 us
    all_to_all x1, starting transfers between devices, shards(): lax.all_to_all(outbound[0], 'seq', split_axis=1, concat_axis=1, tiled=True)  5.64 us
  transfers between devices with their start and end apart: 3, of which 1 were waited for; matrix products, arithmetic and copies ran while one was open for 29% of the time, Pallas kernels for 0%

commit v1 on v0

v1 whole, which is shorter than its diff:
```python
import functools

import jax
import jax.numpy as jnp
from jax import lax
from jax.experimental import pallas as pl
from jax.experimental.pallas import tpu as pltpu
from jax.sharding import PartitionSpec as P

ROPE = 64
LANES = 128
SUBLANES = 8
STAT_ROWS = 16


score_scale = 192.0 ** (-0.5)
masked_value = -1e30
lowest_peak = -1e29
SEARCH_STEPS = 8
SEARCH_WAYS = 8

F32 = jnp.float32
BF16 = jnp.bfloat16


def vmem():
    return pl.BlockSpec(memory_space=pltpu.VMEM)


def smem():
    return pl.BlockSpec(memory_space=pltpu.SMEM)


def dot_nt(a, b):
    return lax.dot_general(a, b, (((1,), (1,)), ((), ())), preferred_element_type=F32)


def query_rows(width, rows):
    full, rest = divmod(width, LANES)
    return full * rows + (rows * rest) // LANES


def pack_kernel(query_ref, index_query_ref, index_weight_ref, out_ref):
    steps, _, heads, width = query_ref.shape
    index_heads = index_query_ref.shape[2]
    rows = steps * heads
    full, rest = divmod(width, LANES)
    for step in range(steps):
        for chunk in range(full):
            out_ref[chunk * rows + step * heads : chunk * rows + (step + 1) * heads, :] = query_ref[
                step, 0, :, chunk * LANES : (chunk + 1) * LANES
            ]
    at = full * rows
    if rest:
        fold = LANES // rest
        tail = jnp.concatenate(
            [query_ref[step, 0, :, full * LANES :] for step in range(steps)], axis=0
        )
        count = rows // fold
        out_ref[at : at + count, :] = jnp.concatenate(
            [tail[part * count : (part + 1) * count] for part in range(fold)], axis=1
        )
        at += count
    for step in range(steps):
        out_ref[at : at + index_heads, :] = index_query_ref[step, 0]
        at += index_heads
    weights = jnp.concatenate([index_weight_ref[step].astype(F32) for step in range(steps)], axis=1)
    out_ref[at : at + STAT_ROWS, :] = jnp.broadcast_to(
        weights, (STAT_ROWS, weights.shape[1])
    ).astype(BF16)


def pack_queries(query, index_query, index_weight):
    steps, _, heads, width = query.shape
    index_rows = steps * index_query.shape[2]
    rows = query_rows(width, steps * heads) + index_rows + STAT_ROWS
    return pl.pallas_call(
        pack_kernel,
        out_shape=jax.ShapeDtypeStruct((rows, LANES), BF16),
        in_specs=[vmem()] * 3,
        out_specs=vmem(),
        name="pack_queries",
    )(query, index_query, index_weight)


def bias_kernel(selected_ref, bias_ref):
    requests, steps, shard_rows = bias_ref.shape
    first = lax.axis_index("seq") * shard_rows
    chunks = shard_rows // LANES
    high_rows = -(-chunks // SUBLANES) * SUBLANES
    count = selected_ref.shape[2]
    for request in range(requests):
        for step in range(steps):
            local = selected_ref[step, request : request + 1, :] - first
            high = local >> 7
            low = local & (LANES - 1)
            high_hot = (lax.broadcasted_iota(jnp.int32, (high_rows, count), 0) == high).astype(F32)
            low_hot = (lax.broadcasted_iota(jnp.int32, (LANES, count), 0) == low).astype(F32)
            hits = dot_nt(high_hot.astype(BF16), low_hot.astype(BF16))
            bias = jnp.where(hits > 0.5, 0.0, masked_value)
            for chunk in range(chunks):
                bias_ref[request, step : step + 1, chunk * LANES : (chunk + 1) * LANES] = bias[
                    chunk : chunk + 1, :
                ]


def selection_bias(selected, shard_rows):
    steps, requests, count = selected.shape
    return pl.pallas_call(
        bias_kernel,
        out_shape=jax.ShapeDtypeStruct((requests, steps, shard_rows), F32),
        in_specs=[vmem()],
        out_specs=vmem(),
        cost_estimate=pl.CostEstimate(
            flops=2 * requests * steps * count * LANES * 16,
            bytes_accessed=requests * steps * (count + shard_rows) * 4,
            transcendentals=0,
        ),
        name="selection_bias",
    )(selected)


def split_three(x):
    high = x.astype(BF16).astype(F32)
    middle = (x - high).astype(BF16).astype(F32)
    return high, middle, x - high - middle


def shard_kernel(seq_count, *refs):
    (owners_ref, lengths_ref), refs = refs[:2], refs[2:]
    sources, refs = refs[:seq_count], refs[seq_count:]
    (key_ref, scale_ref, bias_ref, cache_ref), refs = refs[:4], refs[4:]
    (scores_ref, own_ref, own_stats_ref), refs = refs[:3], refs[3:]
    sends, refs = refs[: seq_count - 1], refs[seq_count - 1 :]
    cache_buf, query_buf, index_buf, candidate_buf, sems = refs

    rank = lax.axis_index("seq")
    requests, width, shard_rows = cache_buf.shape
    steps = scores_ref.shape[0]
    rows = query_buf.shape[1]
    latent = own_ref.shape[1]
    index_rows = index_buf.shape[1] - STAT_ROWS
    index_heads = index_rows // steps
    full, rest = divmod(width, LANES)
    chunks = shard_rows // LANES

    copies = [
        pltpu.make_async_copy(cache_ref.at[request], cache_buf.at[request], sems.at[request])
        for request in range(requests)
    ]
    for copy in copies:
        copy.start()

    for request in range(requests):
        for index, source in enumerate(sources):

            @pl.when(owners_ref[request] == (rank ^ index))
            def _(request=request, source=source):
                for chunk in range(full):
                    query_buf[request, :, chunk * LANES : (chunk + 1) * LANES] = source[
                        chunk * rows : (chunk + 1) * rows, :
                    ]
                at = full * rows
                if rest:
                    fold = LANES // rest
                    count = rows // fold
                    for part in range(fold):
                        query_buf[request, part * count : (part + 1) * count, full * LANES :] = source[
                            at : at + count, part * rest : (part + 1) * rest
                        ]
                    at += count
                index_buf[request] = source[at : at + index_rows + STAT_ROWS, :]

    for request in range(requests):
        dots = dot_nt(index_buf[request, :index_rows, :], key_ref[request])
        weight_row = index_buf[request, index_rows:, :].astype(F32)[:1]
        weight = jnp.transpose(jnp.broadcast_to(weight_row, (LANES, index_rows)))[:, :1]
        terms = jax.nn.relu(dots) * weight
        summed = jnp.concatenate(
            [
                jnp.sum(terms[step * index_heads : (step + 1) * index_heads], axis=0, keepdims=True)
                for step in range(steps)
            ],
            axis=0,
        )
        scores = summed * scale_ref[request : request + 1, :]
        positions = rank * shard_rows + lax.broadcasted_iota(jnp.int32, (steps, shard_rows), 1)
        limit = lengths_ref[request] + lax.broadcasted_iota(jnp.int32, (steps, shard_rows), 0)
        in_length = positions < limit
        scores_ref[:, request, :] = jnp.where(in_length, scores, 0.0)
        candidates = jnp.where(in_length, scores, masked_value)
        for chunk in range(chunks):
            at = (chunk * requests + request) * steps
            candidate_buf[at : at + steps, :] = candidates[:, chunk * LANES : (chunk + 1) * LANES]

    latent_rows = (latent // LANES) * rows
    for request in range(requests):
        copies[request].wait()
        logits = jnp.dot(query_buf[request], cache_buf[request], preferred_element_type=F32)
        bias = jnp.concatenate(
            [
                jnp.broadcast_to(bias_ref[request, step : step + 1, :], (rows // steps, shard_rows))
                for step in range(steps)
            ],
            axis=0,
        )
        logits = logits * score_scale + bias
        peak = jnp.maximum(jnp.max(logits, axis=1, keepdims=True), lowest_peak)
        weights = jnp.exp(logits - peak)
        total = jnp.sum(weights, axis=1, keepdims=True)
        mixture = dot_nt(weights.astype(BF16), cache_buf[request, :latent, :])
        lane = lax.broadcasted_iota(jnp.int32, (rows, LANES), 1)
        stats = jnp.zeros((rows, LANES), F32)
        for index, value in enumerate((*split_three(peak), *split_three(total), peak, total)):
            stats = jnp.where(lane == index, value, stats)
        stats = jnp.transpose(stats)[:STAT_ROWS]

        @pl.when(owners_ref[request] == rank)
        def _(mixture=mixture, stats=stats):
            own_ref[...] = mixture
            own_stats_ref[...] = stats

        packed = mixture.astype(BF16)
        for index, send in enumerate(sends):

            @pl.when(owners_ref[request] == (rank ^ (index + 1)))
            def _(send=send, packed=packed, stats=stats):
                for chunk in range(latent // LANES):
                    send[chunk * rows : (chunk + 1) * rows, :] = packed[
                        :, chunk * LANES : (chunk + 1) * LANES
                    ]
                send[latent_rows : latent_rows + STAT_ROWS, :] = stats.astype(BF16)

    own_candidates = candidate_buf[...].astype(BF16)
    for send in sends:
        send[latent_rows + STAT_ROWS :, :] = own_candidates


def shard_sums(owners, lengths, sources, index_key, index_scale, bias, cache_t, latent):
    seq_count = len(sources)
    requests, width, shard_rows = cache_t.shape
    steps = bias.shape[1]
    rows = LANES
    index_block = sources[0].shape[0] - query_rows(width, rows)
    candidate_rows = requests * steps * (shard_rows // LANES)
    send_rows = (latent // LANES) * rows + STAT_ROWS + candidate_rows
    return pl.pallas_call(
        functools.partial(shard_kernel, seq_count),
        out_shape=(
            jax.ShapeDtypeStruct((steps, requests, shard_rows), F32),
            jax.ShapeDtypeStruct((rows, latent), F32),
            jax.ShapeDtypeStruct((STAT_ROWS, LANES), F32),
        )
        + (jax.ShapeDtypeStruct((send_rows, LANES), BF16),) * (seq_count - 1),
        in_specs=[smem()] * 2 + [vmem()] * (seq_count + 3) + [pl.BlockSpec(memory_space=pl.ANY)],
        out_specs=(vmem(),) * (seq_count + 2),
        scratch_shapes=[
            pltpu.VMEM((requests, width, shard_rows), BF16),
            pltpu.VMEM((requests, rows, width), BF16),
            pltpu.VMEM((requests, index_block, LANES), BF16),
            pltpu.VMEM((candidate_rows, LANES), F32),
            pltpu.SemaphoreType.DMA((requests,)),
        ],
        name="shard_sums",
    )(owners, lengths, *sources, index_key, index_scale, bias, cache_t)


def search_threshold(pieces, lists, keep_count):
    group = max(lists, SUBLANES)
    values = jnp.concatenate(pieces, axis=0)
    values = values.reshape(values.shape[0] // group, group, LANES)

    def across(x, join, lane_join):
        x = lane_join(x, axis=1, keepdims=True)
        shift = lists
        x = jnp.broadcast_to(x, (group, LANES))
        while shift < group:
            x = join(x, pltpu.roll(x, shift, 0))
            shift *= 2
        return x

    low = across(
        jnp.min(jnp.where(values > lowest_peak, values, -masked_value), axis=0), jnp.minimum, jnp.min
    )
    high = across(jnp.max(values, axis=0), jnp.maximum, jnp.max)
    for _ in range(SEARCH_STEPS):
        width = (high - low) * (1.0 / SEARCH_WAYS)
        new_low, new_high = low, high
        for way in range(1, SEARCH_WAYS):
            middle = low + width * way
            count = across(
                jnp.sum((values >= middle[None]).astype(F32), axis=0), jnp.add, jnp.sum
            )
            enough = count >= keep_count
            new_low = jnp.where(enough, jnp.maximum(new_low, middle), new_low)
            new_high = jnp.where(enough, new_high, jnp.minimum(new_high, middle))
        low, high = new_low, new_high
    return across(
        jnp.min(jnp.where(values >= low[None], values, -masked_value), axis=0),
        jnp.minimum,
        jnp.min,
    )


def merge_kernel(seq_count, keep_count, *refs):
    owners_ref, own_ref, own_stats_ref, own_candidates_ref = refs[:4]
    received = refs[4 : 4 + seq_count - 1]
    threshold_ref, attended_ref = refs[4 + seq_count - 1 :]
    rank = lax.axis_index("seq")
    rows, latent = own_ref.shape
    steps, requests = threshold_ref.shape
    latent_rows = (latent // LANES) * rows
    first_candidate = latent_rows + STAT_ROWS

    pieces = [own_candidates_ref[first_candidate:, :].astype(F32)]
    pieces += [ref[first_candidate:, :].astype(F32) for ref in received]
    threshold = search_threshold(pieces, steps * requests, keep_count)
    for request in range(requests):
        for step in range(steps):
            at = request * steps + step
            threshold_ref[step : step + 1, request : request + 1] = threshold[at : at + 1, :1]

    def stat_columns(ref_rows):
        block = jnp.concatenate(
            [ref_rows, jnp.zeros((LANES - ref_rows.shape[0], LANES), F32)], axis=0
        )
        return jnp.transpose(block)

    own_stats = own_stats_ref[...]
    columns = stat_columns(own_stats)
    peaks = [columns[:, 6:7]]
    totals = [columns[:, 7:8]]
    for ref in received:
        columns = stat_columns(ref[latent_rows : latent_rows + STAT_ROWS, :].astype(F32))
        peaks.append(columns[:, 0:1] + columns[:, 1:2] + columns[:, 2:3])
        totals.append(columns[:, 3:4] + columns[:, 4:5] + columns[:, 5:6])
    highest = functools.reduce(jnp.maximum, peaks)
    factors = [jnp.exp(peak - highest) for peak in peaks]
    total = functools.reduce(jnp.add, [a * b for a, b in zip(totals, factors)])
    factors = [factor / total for factor in factors]
    holds = functools.reduce(
        jnp.logical_or, [owners_ref[request] == rank for request in range(requests)]
    )
    heads = rows // steps

    @pl.when(holds)
    def _():
        for chunk in range(latent // LANES):
            part = slice(chunk * LANES, (chunk + 1) * LANES)
            merged = own_ref[:, part] * factors[0]
            for ref, factor in zip(received, factors[1:]):
                merged += ref[chunk * rows : (chunk + 1) * rows, :].astype(F32) * factor
            merged = merged.astype(BF16)
            for step in range(steps):
                attended_ref[step, 0, :, part] = merged[step * heads : (step + 1) * heads]

    @pl.when(jnp.logical_not(holds))
    def _():
        attended_ref[...] = jnp.zeros_like(attended_ref)


def merge(owners, own, own_stats, own_send, received, steps, requests, keep_count):
    seq_count = len(received) + 1
    rows, latent = own.shape
    return pl.pallas_call(
        functools.partial(merge_kernel, seq_count, keep_count),
        out_shape=(
            jax.ShapeDtypeStruct((steps, requests), F32),
            jax.ShapeDtypeStruct((steps, 1, rows // steps, latent), BF16),
        ),
        in_specs=[smem()] + [vmem()] * (seq_count + 2),
        out_specs=(vmem(), vmem()),
        name="merge",
    )(owners, own, own_stats, own_send, *received)


def shards(
    cache, index_key, index_scale, lengths, owners, selected, query, index_query, index_weight
):
    seq_count = lax.axis_size("seq")
    requests, shard_rows, width = cache.shape
    steps, _, keep_count = selected.shape
    latent = width - ROPE
    cache_t = jnp.transpose(cache, (0, 2, 1))

    def exchange(x, bit):
        return lax.ppermute(x, "seq", [(place, place ^ bit) for place in range(seq_count)])

    packed = pack_queries(query, index_query, index_weight)
    sources = [packed] + [exchange(packed, bit) for bit in range(1, seq_count)]
    bias = selection_bias(selected, shard_rows)
    index_scores, own, own_stats, *sends = shard_sums(
        owners, lengths, sources, index_key, index_scale, bias, cache_t, latent
    )
    received = [exchange(send, bit) for bit, send in enumerate(sends, 1)]
    threshold, attended = merge(
        owners, own, own_stats, sends[0], received, steps, requests, keep_count
    )
    return (index_scores, threshold, attended)


def solution(mesh):
    placed = (
        P(("groups", "req"), "seq", None),
        P(("groups", "req"), "seq", None),
        P(("groups", "req"), "seq"),
        P(("groups", "req")),
        P(("groups", "req")),
        P(None, ("groups", "req"), None),
        P(None, ("groups", "seq", "req"), "head", None),
        P(None, ("groups", "seq", "req"), None, None),
        P(None, ("groups", "seq", "req"), None),
    )
    return jax.shard_map(
        shards,
        mesh=mesh,
        in_specs=placed,
        out_specs=(
            P(None, ("groups", "req"), "seq"),
            P(None, ("groups", "req")),
            P(None, ("groups", "seq", "req"), "head", None),
        ),
        check_vma=False,
    )
```

time: 211 us -> 49.6 us (0.24)
  local copies, waits for them, and re-layouts: 66.4 us -> 2.6 us
  other arithmetic: 62.7 us -> 0 us
  blocking collectives: 57.6 us -> 0 us
  waiting for transfers between devices: 4.14 us -> 23.2 us
  Pallas kernels: 0 us -> 13.7 us
  matrix products: 5.33 us -> 0 us
  starting transfers between devices: 12.7 us -> 9.19 us
    all_gather x4 -> x0, blocking collectives: 57.6 us -> none  [the longest x1 19.7 us: shards(): all_queries = lax.all_gather(query, 'seq', axis=1, tiled=True)]
    top_k x3 -> x0, other arithmetic: 49.5 us -> none  [top_values(): return lax.top_k(jnp.concatenate([earlier, later], axis=-1), keep_count)[0]]
    unnamed x26 -> x13, local copies, waits for them, and re-layouts: 40.3 us -> 2.6 us
    gather x5 -> x0, local copies, waits for them, and re-layouts: 24.3 us -> none  [the longest x2 22.6 us: shards(): jnp.take(flat_cache, request_ids[None, :, None] * shard_rows + slot_posit...]
    ppermute x0 -> x6, waiting for transfers between devices: none -> 23.2 us  [exchange(): lax.ppermute(x, 'seq', [(place, place ^ bit) for place in range(seq_count)])]
    pallas_call x0 -> x4, Pallas kernels: none -> 13.7 us  [the longest x1 6.16 us: shard_sums(): pl.pallas_call(functools.partial(shard_kernel, seq_count), out_shape=(jax...]
    all_to_all x3 -> x0, starting transfers between devices: 12.7 us -> none  [the longest x1 5.64 us: shards(): lax.all_to_all(outbound[0], 'seq', split_axis=1, concat_axis=1, tiled=True)]
    ppermute x0 -> x6, starting transfers between devices: none -> 9.19 us  [exchange(): lax.ppermute(x, 'seq', [(place, place ^ bit) for place in range(seq_count)])]
  transfers between devices with their start and end apart: 3 -> 6, of which waited for: 1 -> 4; matrix products, arithmetic and copies ran while one was open for 29% -> 0% of each run, Pallas kernels for 0% -> 4%
where the time goes in v1:
time: 49.6 us; the launch traced here: 49.4 us
  waiting for transfers between devices  23.2 us (47%)
  Pallas kernels  13.7 us (28%)
  starting transfers between devices  9.19 us (19%)
  local copies, waits for them, and re-layouts  2.6 us (5%)
  between operations  0.66 us (1%)
    ppermute x6, waiting for transfers between devices, exchange(): lax.ppermute(x, 'seq', [(place, place ^ bit) for place in range(seq_count)])  23.2 us
    ppermute x6, starting transfers between devices, exchange(): lax.ppermute(x, 'seq', [(place, place ^ bit) for place in range(seq_count)])  9.19 us
    pallas_call x1, Pallas kernels, shard_sums(): pl.pallas_call(functools.partial(shard_kernel, seq_count), out_shape=(jax...  6.16 us
    pallas_call x1, Pallas kernels, merge(): pl.pallas_call(functools.partial(merge_kernel, seq_count, keep_count), ou...  3.86 us
    unnamed x13, local copies, waits for them, and re-layouts  2.6 us
    pallas_call x1, Pallas kernels, selection_bias(): pl.pallas_call(bias_kernel, out_shape=jax.ShapeDtypeStruct((requests, ste...  2.04 us
    pallas_call x1, Pallas kernels, pack_queries(): pl.pallas_call(pack_kernel, out_shape=jax.ShapeDtypeStruct((rows, LANES),...  1.69 us
  transfers between devices with their start and end apart: 6, of which 4 were waited for; matrix products, arithmetic and copies ran while one was open for 0% of the time, Pallas kernels for 4%

profile of v1, /device:TPU:0, one launch (start us, length us, event | category | flops | bytes accessed | tf_op | source)
XLA Modules:
  0.0 49.4 jit_solution(18181490000255959089)
XLA Ops:
  0.6 1.2 %copy.12.index_weight_ref = bf16[2,1,64]{2,1,0:T(2,128)(2,1)} copy(bf16[2,1,64]{2,0,1:T(2,128)(2,1)} %param.17) | data formatting | bytes 512 | tf_op args[8]
  1.9 1.7 %pack_queries.1.refs_2_ = bf16[720,128]{1,0:T(8,128)(2,1)} custom-call(bf16[2,1,64,576]{3,2,1,0:T(8,128)(2,1)} %query_ref.1, bf16[2,1,64,128]{3,2,1,0:T(8,128)(2,1)} %index_query_ref.1, bf16[2,1,64]{2,1,0:T(2,128)(2,1)} %copy.12.index_weight_ref), custom_call_target="tpu_custom_call" | custom-call | tf_op jit(solution)/shard_map/pack_queries/pallas_call | solution.py:77
  3.5 5.1 %collective-permute-start.2 = (bf16[720,128]{1,0:T(8,128)(2,1)}, bf16[720,128]{1,0:T(8,128)(2,1)S(1)}, u32[]{:S(2)}, u32[]{:S(2)}) collective-permute-start(bf16[720,128]{1,0:T(8,128)(2,1)} %pack_queries.1.refs_2_), channel_id=1, source_target_pairs={{0,12},{4,8},{8,4},{12,0},{1,13},{5,9},{9,5},{13,1},{2,14},{6,10},... | collective-permute-start | bytes 552968 | tf_op jit(solution)/shard_map/ppermute | solution.py:387
  8.6 0.0 collective-permute-start.1
  8.6 0.6 %collective-permute-start = (bf16[720,128]{1,0:T(8,128)(2,1)}, bf16[720,128]{1,0:T(8,128)(2,1)S(1)}, u32[]{:S(2)}, u32[]{:S(2)}) collective-permute-start(bf16[720,128]{1,0:T(8,128)(2,1)} %pack_queries.1.refs_2_), channel_id=1, source_target_pairs={{0,4},{4,0},{8,12},{12,8},{1,5},{5,1},{9,13},{13,9},{2,6},{6,2},{1... | collective-permute-start | bytes 552968 | tf_op jit(solution)/shard_map/ppermute | solution.py:387
  9.2 2.0 %selection_bias.1.refs_8_ = f32[2,2,1536]{2,1,0:T(2,128)} custom-call(s32[2,2,2048]{2,1,0:T(2,128)} %selected_ref.1), custom_call_target="tpu_custom_call" | custom-call | flops 33554432 | bytes 57344 | tf_op jit(solution)/shard_map/selection_bias/pallas_call | solution.py:109
  11.2 3.2 %collective-permute-done.2.refs_5_ = bf16[720,128]{1,0:T(8,128)(2,1)S(1)} collective-permute-done((bf16[720,128]{1,0:T(8,128)(2,1)}, bf16[720,128]{1,0:T(8,128)(2,1)S(1)}, u32[]{:S(2)}, u32[]{:S(2)}) %collective-permute-start.2) | collective-permute-done | bytes 184352 | tf_op jit(solution)/shard_map/ppermute | solution.py:387
  14.4 0.0 copy-start
  14.4 10.0 %collective-permute-done.1.refs_4_ = bf16[720,128]{1,0:T(8,128)(2,1)S(1)} collective-permute-done((bf16[720,128]{1,0:T(8,128)(2,1)}, bf16[720,128]{1,0:T(8,128)(2,1)S(1)}, u32[]{:S(2)}, u32[]{:S(2)}) %collective-permute-start.1) | collective-permute-done | bytes 184352 | tf_op jit(solution)/shard_map/ppermute | solution.py:387
  24.5 0.0 copy-start.1
  24.5 0.0 collective-permute-done.refs_3_
  24.5 0.0 copy-start.2
  24.5 0.0 copy-done
  24.5 0.7 %copy-done.1 = bf16[720,128]{1,0:T(8,128)(2,1)} copy-done((bf16[720,128]{1,0:T(8,128)(2,1)}, bf16[720,128]{1,0:T(8,128)(2,1)S(1)}, u32[]{:S(2)}) %copy-start.1) | copy-done | bytes 184344
  25.1 0.1 copy-done.2
  25.2 6.2 %shard_sums.1 = (f32[2,2,1536]{2,1,0:T(2,128)}, f32[128,512]{1,0:T(8,128)}, f32[16,128]{1,0:T(8,128)}, bf16[576,128]{1,0:T(8,128)(2,1)}, bf16[576,128]{1,0:T(8,128)(2,1)}, /*index=5*/bf16[576,128]{1,0:T(8,128)(2,1)}) custom-call(s32[2]{0:T(128)} %refs_0_.3, s32[2]{0:T(128)} %refs_1_.1, bf16[720,128]{1,0:T(8,128)(2,1)} %pack_queries.1.refs_2_, ...), custom_call_target="tpu_custom_call" | custom-call | tf_op jit(solution)/shard_map/shard_sums/pallas_call | solution.py:247
  31.4 0.1 collective-permute-start.4
  31.5 2.5 %collective-permute-start.5 = (bf16[576,128]{1,0:T(8,128)(2,1)}, bf16[576,128]{1,0:T(8,128)(2,1)S(1)}, u32[]{:S(2)}, u32[]{:S(2)}) collective-permute-start(bf16[576,128]{1,0:T(8,128)(2,1)} %get-tuple-element.16), channel_id=1, source_target_pairs={{0,12},{4,8},{8,4},{12,0},{1,13},{5,9},{9,5},{13,1},{2,14},{6,10},... | collective-permute-start | bytes 442376 | tf_op jit(solution)/shard_map/ppermute | solution.py:387
  34.0 0.9 %collective-permute-start.3 = (bf16[576,128]{1,0:T(8,128)(2,1)}, bf16[576,128]{1,0:T(8,128)(2,1)S(1)}, u32[]{:S(2)}, u32[]{:S(2)}) collective-permute-start(bf16[576,128]{1,0:T(8,128)(2,1)} %get-tuple-element.14.refs_3_), channel_id=1, source_target_pairs={{0,4},{4,0},{8,12},{12,8},{1,5},{5,1},{9,13},{13,9},{2,6},{6,2},{1... | collective-permute-start | bytes 442376 | tf_op jit(solution)/shard_map/ppermute | solution.py:387
  34.9 8.6 %collective-permute-done.4.refs_5_ = bf16[576,128]{1,0:T(8,128)(2,1)S(1)} collective-permute-done((bf16[576,128]{1,0:T(8,128)(2,1)}, bf16[576,128]{1,0:T(8,128)(2,1)S(1)}, u32[]{:S(2)}, u32[]{:S(2)}) %collective-permute-start.4) | collective-permute-done | bytes 147488 | tf_op jit(solution)/shard_map/ppermute | solution.py:387
  43.6 0.0 copy-start.3
  43.6 0.0 collective-permute-done.5.refs_6_
  43.6 0.0 copy-start.4
  43.6 1.3 %collective-permute-done.3.refs_4_ = bf16[576,128]{1,0:T(8,128)(2,1)S(1)} collective-permute-done((bf16[576,128]{1,0:T(8,128)(2,1)}, bf16[576,128]{1,0:T(8,128)(2,1)S(1)}, u32[]{:S(2)}, u32[]{:S(2)}) %collective-permute-start.3) | collective-permute-done | bytes 147488 | tf_op jit(solution)/shard_map/ppermute | solution.py:387
  44.9 0.0 copy-start.5
  44.9 0.0 copy-done.3
  44.9 0.0 copy-done.4
  44.9 0.6 %copy-done.5 = bf16[576,128]{1,0:T(8,128)(2,1)} copy-done((bf16[576,128]{1,0:T(8,128)(2,1)}, bf16[576,128]{1,0:T(8,128)(2,1)S(1)}, u32[]{:S(2)}) %copy-start.5) | copy-done | bytes 147480
  45.5 3.9 %merge.1 = (f32[2,2]{1,0:T(2,128)}, bf16[2,1,64,512]{3,2,1,0:T(8,128)(2,1)}) custom-call(s32[2]{0:T(128)} %refs_0_.3, f32[128,512]{1,0:T(8,128)} %get-tuple-element.12.refs_1_, f32[16,128]{1,0:T(8,128)} %get-tuple-element.13.refs_2_, bf16[576,128]{1,0:T(8,128)(2,1)} %get-tuple-element.14.refs_3_, bf16[576,128]{1,0:T(8,128)(2,1)} %copy-done.5, ...), custom_call_target="tpu_custom_call" | custom-call | tf_op jit(solution)/shard_map/merge/pallas_call | solution.py:365
Async XLA Ops:
  3.5 10.9 %collective-permute-start.2 = (bf16[720,128]{1,0:T(8,128)(2,1)}, bf16[720,128]{1,0:T(8,128)(2,1)S(1)}, u32[]{:S(2)}, u32[]{:S(2)}) collective-permute-start(bf16[720,128]{1,0:T(8,128)(2,1)} %pack_queries.1.refs_2_), channel_id=1, source_target_pairs={{0,12},{4,8},{8,4},{12,0},{1,13},{5,9},{9,5},{13,1},{2,14},{6,10},... | collective-permute-start | bytes 552968 | tf_op jit(solution)/shard_map/ppermute | solution.py:387
  8.6 15.8 %collective-permute-start.1 = (bf16[720,128]{1,0:T(8,128)(2,1)}, bf16[720,128]{1,0:T(8,128)(2,1)S(1)}, u32[]{:S(2)}, u32[]{:S(2)}) collective-permute-start(bf16[720,128]{1,0:T(8,128)(2,1)} %pack_queries.1.refs_2_), channel_id=1, source_target_pairs={{0,8},{4,12},{8,0},{12,4},{1,9},{5,13},{9,1},{13,5},{2,10},{6,14},... | collective-permute-start | bytes 552968 | tf_op jit(solution)/shard_map/ppermute | solution.py:387
  8.6 15.9 %collective-permute-start = (bf16[720,128]{1,0:T(8,128)(2,1)}, bf16[720,128]{1,0:T(8,128)(2,1)S(1)}, u32[]{:S(2)}, u32[]{:S(2)}) collective-permute-start(bf16[720,128]{1,0:T(8,128)(2,1)} %pack_queries.1.refs_2_), channel_id=1, source_target_pairs={{0,4},{4,0},{8,12},{12,8},{1,5},{5,1},{9,13},{13,9},{2,6},{6,2},{1... | collective-permute-start | bytes 552968 | tf_op jit(solution)/shard_map/ppermute | solution.py:387
  14.4 10.0 %copy-start = (bf16[720,128]{1,0:T(8,128)(2,1)}, bf16[720,128]{1,0:T(8,128)(2,1)S(1)}, u32[]{:S(2)}) copy-start(bf16[720,128]{1,0:T(8,128)(2,1)S(1)} %collective-permute-done.2.refs_5_) | copy-start | bytes 552964
  24.5 0.7 %copy-start.1 = (bf16[720,128]{1,0:T(8,128)(2,1)}, bf16[720,128]{1,0:T(8,128)(2,1)S(1)}, u32[]{:S(2)}) copy-start(bf16[720,128]{1,0:T(8,128)(2,1)S(1)} %collective-permute-done.1.refs_4_) | copy-start | bytes 552964
  24.5 0.7 %copy-start.2 = (bf16[720,128]{1,0:T(8,128)(2,1)}, bf16[720,128]{1,0:T(8,128)(2,1)S(1)}, u32[]{:S(2)}) copy-start(bf16[720,128]{1,0:T(8,128)(2,1)S(1)} %collective-permute-done.refs_3_) | copy-start | bytes 552964
  31.4 12.2 %collective-permute-start.4 = (bf16[576,128]{1,0:T(8,128)(2,1)}, bf16[576,128]{1,0:T(8,128)(2,1)S(1)}, u32[]{:S(2)}, u32[]{:S(2)}) collective-permute-start(bf16[576,128]{1,0:T(8,128)(2,1)} %get-tuple-element.15), channel_id=1, source_target_pairs={{0,8},{4,12},{8,0},{12,4},{1,9},{5,13},{9,1},{13,5},{2,10},{6,14},... | collective-permute-start | bytes 442376 | tf_op jit(solution)/shard_map/ppermute | solution.py:387
  31.5 12.1 %collective-permute-start.5 = (bf16[576,128]{1,0:T(8,128)(2,1)}, bf16[576,128]{1,0:T(8,128)(2,1)S(1)}, u32[]{:S(2)}, u32[]{:S(2)}) collective-permute-start(bf16[576,128]{1,0:T(8,128)(2,1)} %get-tuple-element.16), channel_id=1, source_target_pairs={{0,12},{4,8},{8,4},{12,0},{1,13},{5,9},{9,5},{13,1},{2,14},{6,10},... | collective-permute-start | bytes 442376 | tf_op jit(solution)/shard_map/ppermute | solution.py:387
  34.0 10.9 %collective-permute-start.3 = (bf16[576,128]{1,0:T(8,128)(2,1)}, bf16[576,128]{1,0:T(8,128)(2,1)S(1)}, u32[]{:S(2)}, u32[]{:S(2)}) collective-permute-start(bf16[576,128]{1,0:T(8,128)(2,1)} %get-tuple-element.14.refs_3_), channel_id=1, source_target_pairs={{0,4},{4,0},{8,12},{12,8},{1,5},{5,1},{9,13},{13,9},{2,6},{6,2},{1... | collective-permute-start | bytes 442376 | tf_op jit(solution)/shard_map/ppermute | solution.py:387
  43.6 1.3 %copy-start.3 = (bf16[576,128]{1,0:T(8,128)(2,1)}, bf16[576,128]{1,0:T(8,128)(2,1)S(1)}, u32[]{:S(2)}) copy-start(bf16[576,128]{1,0:T(8,128)(2,1)S(1)} %collective-permute-done.4.refs_5_) | copy-start | bytes 442372
  43.6 1.3 %copy-start.4 = (bf16[576,128]{1,0:T(8,128)(2,1)}, bf16[576,128]{1,0:T(8,128)(2,1)S(1)}, u32[]{:S(2)}) copy-start(bf16[576,128]{1,0:T(8,128)(2,1)S(1)} %collective-permute-done.5.refs_6_) | copy-start | bytes 442372
  44.9 0.6 %copy-start.5 = (bf16[576,128]{1,0:T(8,128)(2,1)}, bf16[576,128]{1,0:T(8,128)(2,1)S(1)}, u32[]{:S(2)}) copy-start(bf16[576,128]{1,0:T(8,128)(2,1)S(1)} %collective-permute-done.3.refs_4_) | copy-start | bytes 442372

commit v2 on v1

--- a/solution.py
+++ b/solution.py
@@ -11,6 +11,7 @@
 LANES = 128
 SUBLANES = 8
 STAT_ROWS = 16
+VMEM_GRANT = 12 * 2**20
 
 
 score_scale = 192.0 ** (-0.5)
@@ -29,6 +30,10 @@
 
 def smem():
     return pl.BlockSpec(memory_space=pltpu.SMEM)
+
+
+def grant():
+    return pltpu.CompilerParams(vmem_limit_bytes=VMEM_GRANT)
 
 
 def dot_nt(a, b):
@@ -64,7 +69,7 @@
     for step in range(steps):
         out_ref[at : at + index_heads, :] = index_query_ref[step, 0]
         at += index_heads
-    weights = jnp.concatenate([index_weight_ref[step].astype(F32) for step in range(steps)], axis=1)
+    weights = jnp.concatenate([index_weight_ref[:, step].astype(F32) for step in range(steps)], axis=1)
     out_ref[at : at + STAT_ROWS, :] = jnp.broadcast_to(
         weights, (STAT_ROWS, weights.shape[1])
     ).astype(BF16)
@@ -79,11 +84,14 @@
         out_shape=jax.ShapeDtypeStruct((rows, LANES), BF16),
         in_specs=[vmem()] * 3,
         out_specs=vmem(),
+        compiler_params=grant(),
         name="pack_queries",
     )(query, index_query, index_weight)
 
 
-def bias_kernel(selected_ref, bias_ref):
+def bias_kernel(selected_ref, cache_ref, bias_ref, staged_ref, sem):
+    copy = pltpu.make_async_copy(cache_ref, staged_ref, sem)
+    copy.start()
     requests, steps, shard_rows = bias_ref.shape
     first = lax.axis_index("seq") * shard_rows
     chunks = shard_rows // LANES
@@ -102,22 +110,29 @@
                 bias_ref[request, step : step + 1, chunk * LANES : (chunk + 1) * LANES] = bias[
                     chunk : chunk + 1, :
                 ]
-
-
-def selection_bias(selected, shard_rows):
+    copy.wait()
+
+
+def selection_bias(selected, cache_t):
     steps, requests, count = selected.shape
+    shard_rows = cache_t.shape[2]
     return pl.pallas_call(
         bias_kernel,
-        out_shape=jax.ShapeDtypeStruct((requests, steps, shard_rows), F32),
-        in_specs=[vmem()],
-        out_specs=vmem(),
+        out_shape=(
+            jax.ShapeDtypeStruct((requests, steps, shard_rows), F32),
+            jax.ShapeDtypeStruct(cache_t.shape, cache_t.dtype),
+        ),
+        in_specs=[vmem(), pl.BlockSpec(memory_space=pl.ANY)],
+        out_specs=(vmem(), vmem()),
+        scratch_shapes=[pltpu.SemaphoreType.DMA],
         cost_estimate=pl.CostEstimate(
             flops=2 * requests * steps * count * LANES * 16,
             bytes_accessed=requests * steps * (count + shard_rows) * 4,
             transcendentals=0,
         ),
+        compiler_params=grant(),
         name="selection_bias",
-    )(selected)
+    )(selected, cache_t)
 
 
 def split_three(x):
@@ -132,10 +147,10 @@
     (key_ref, scale_ref, bias_ref, cache_ref), refs = refs[:4], refs[4:]
     (scores_ref, own_ref, own_stats_ref), refs = refs[:3], refs[3:]
     sends, refs = refs[: seq_count - 1], refs[seq_count - 1 :]
-    cache_buf, query_buf, index_buf, candidate_buf, sems = refs
+    query_buf, index_buf, candidate_buf = refs
 
     rank = lax.axis_index("seq")
-    requests, width, shard_rows = cache_buf.shape
+    requests, width, shard_rows = cache_ref.shape
     steps = scores_ref.shape[0]
     rows = query_buf.shape[1]
     latent = own_ref.shape[1]
@@ -143,13 +158,6 @@
     index_heads = index_rows // steps
     full, rest = divmod(width, LANES)
     chunks = shard_rows // LANES
-
-    copies = [
-        pltpu.make_async_copy(cache_ref.at[request], cache_buf.at[request], sems.at[request])
-        for request in range(requests)
-    ]
-    for copy in copies:
-        copy.start()
 
     for request in range(requests):
         for index, source in enumerate(sources):
@@ -195,8 +203,7 @@
 
     latent_rows = (latent // LANES) * rows
     for request in range(requests):
-        copies[request].wait()
-        logits = jnp.dot(query_buf[request], cache_buf[request], preferred_element_type=F32)
+        logits = jnp.dot(query_buf[request], cache_ref[request], preferred_element_type=F32)
         bias = jnp.concatenate(
             [
                 jnp.broadcast_to(bias_ref[request, step : step + 1, :], (rows // steps, shard_rows))
@@ -208,7 +215,7 @@
         peak = jnp.maximum(jnp.max(logits, axis=1, keepdims=True), lowest_peak)
         weights = jnp.exp(logits - peak)
         total = jnp.sum(weights, axis=1, keepdims=True)
-        mixture = dot_nt(weights.astype(BF16), cache_buf[request, :latent, :])
+        mixture = dot_nt(weights.astype(BF16), cache_ref[request, :latent, :])
         lane = lax.broadcasted_iota(jnp.int32, (rows, LANES), 1)
         stats = jnp.zeros((rows, LANES), F32)
         for index, value in enumerate((*split_three(peak), *split_three(total), peak, total)):
@@ -252,15 +259,14 @@
             jax.ShapeDtypeStruct((STAT_ROWS, LANES), F32),
         )
         + (jax.ShapeDtypeStruct((send_rows, LANES), BF16),) * (seq_count - 1),
-        in_specs=[smem()] * 2 + [vmem()] * (seq_count + 3) + [pl.BlockSpec(memory_space=pl.ANY)],
+        in_specs=[smem()] * 2 + [vmem()] * (seq_count + 4),
         out_specs=(vmem(),) * (seq_count + 2),
         scratch_shapes=[
-            pltpu.VMEM((requests, width, shard_rows), BF16),
             pltpu.VMEM((requests, rows, width), BF16),
             pltpu.VMEM((requests, index_block, LANES), BF16),
             pltpu.VMEM((candidate_rows, LANES), F32),
-            pltpu.SemaphoreType.DMA((requests,)),
         ],
+        compiler_params=grant(),
         name="shard_sums",
     )(owners, lengths, *sources, index_key, index_scale, bias, cache_t)
 
@@ -370,6 +376,7 @@
         ),
         in_specs=[smem()] + [vmem()] * (seq_count + 2),
         out_specs=(vmem(), vmem()),
+        compiler_params=grant(),
         name="merge",
     )(owners, own, own_stats, own_send, *received)
 
@@ -386,11 +393,11 @@
     def exchange(x, bit):
         return lax.ppermute(x, "seq", [(place, place ^ bit) for place in range(seq_count)])
 
-    packed = pack_queries(query, index_query, index_weight)
+    packed = pack_queries(query, index_query, jnp.transpose(index_weight, (1, 0, 2)))
     sources = [packed] + [exchange(packed, bit) for bit in range(1, seq_count)]
-    bias = selection_bias(selected, shard_rows)
+    bias, staged = selection_bias(selected, cache_t)
     index_scores, own, own_stats, *sends = shard_sums(
-        owners, lengths, sources, index_key, index_scale, bias, cache_t, latent
+        owners, lengths, sources, index_key, index_scale, bias, staged, latent
     )
     received = [exchange(send, bit) for bit, send in enumerate(sends, 1)]
     threshold, attended = merge(

time: 49.6 us -> 44.5 us (0.90)
  Pallas kernels: 13.7 us -> 8.41 us
  local copies, waits for them, and re-layouts: 2.6 us -> 5.11 us
  waiting for transfers between devices: 23.2 us -> 20.8 us
    unnamed x13 -> x18, local copies, waits for them, and re-layouts: 2.6 us -> 5.11 us
    ppermute x6, waiting for transfers between devices: 23.2 us -> 20.8 us  [exchange(): lax.ppermute(x, 'seq', [(place, place ^ bit) for place in range(seq_count)])]
    pallas_call x1, Pallas kernels: 6.16 us -> 4.03 us  [shard_sums(): pl.pallas_call(functools.partial(shard_kernel, seq_count), out_shape=(jax...]
    pallas_call x1, Pallas kernels: 1.69 us -> 0.1 us  [pack_queries(): pl.pallas_call(pack_kernel, out_shape=jax.ShapeDtypeStruct((rows, LANES),...]
    pallas_call x1, Pallas kernels: 2.04 us -> 1.08 us  [selection_bias(): pl.pallas_call(bias_kernel, out_shape=(jax.ShapeDtypeStruct((requests, st...]
    pallas_call x1, Pallas kernels: 3.86 us -> 3.19 us  [merge(): pl.pallas_call(functools.partial(merge_kernel, seq_count, keep_count), ou...]
  transfers between devices with their start and end apart: 6 -> 6, of which waited for: 4 -> 4; matrix products, arithmetic and copies ran while one was open for 0% -> 0% of each run, Pallas kernels for 4% -> 2%
where the time goes in v2:
time: 44.5 us; the launch traced here: 44.2 us
  waiting for transfers between devices  20.8 us (47%)
  starting transfers between devices  9.23 us (21%)
  Pallas kernels  8.41 us (19%)
  local copies, waits for them, and re-layouts  5.11 us (11%)
  between operations  0.7 us (2%)
    ppermute x6, waiting for transfers between devices, exchange(): lax.ppermute(x, 'seq', [(place, place ^ bit) for place in range(seq_count)])  20.8 us
    ppermute x6, starting transfers between devices, exchange(): lax.ppermute(x, 'seq', [(place, place ^ bit) for place in range(seq_count)])  9.23 us
    unnamed x18, local copies, waits for them, and re-layouts  5.11 us
    pallas_call x1, Pallas kernels, shard_sums(): pl.pallas_call(functools.partial(shard_kernel, seq_count), out_shape=(jax...  4.03 us
    pallas_call x1, Pallas kernels, merge(): pl.pallas_call(functools.partial(merge_kernel, seq_count, keep_count), ou...  3.19 us
    pallas_call x1, Pallas kernels, selection_bias(): pl.pallas_call(bias_kernel, out_shape=(jax.ShapeDtypeStruct((requests, st...  1.08 us
  transfers between devices with their start and end apart: 6, of which 4 were waited for; matrix products, arithmetic and copies ran while one was open for 0% of the time, Pallas kernels for 2%

profile of v2, /device:TPU:0, one launch (start us, length us, event | category | flops | bytes accessed | tf_op | source)
XLA Modules:
  0.0 44.2 jit_solution(776297000484451751)
XLA Ops:
  0.6 0.0 copy-start.6
  0.6 0.0 copy-start.8
  0.7 0.0 copy-start.2
  0.7 0.9 %copy-done.2 = bf16[2,1,64,576]{3,2,1,0:T(8,128)(2,1)S(1)} copy-done((bf16[2,1,64,576]{3,2,1,0:T(8,128)(2,1)S(1)}, bf16[2,1,64,576]{3,2,1,0:T(8,128)(2,1)}, u32[]{:S(2)}) %copy-start.2) | copy-done | bytes 147480
  1.6 0.0 copy-start.4
  1.6 0.8 %copy-done.4 = bf16[2,1,64,128]{3,2,1,0:T(8,128)(2,1)S(1)} copy-done((bf16[2,1,64,128]{3,2,1,0:T(8,128)(2,1)S(1)}, bf16[2,1,64,128]{3,2,1,0:T(8,128)(2,1)}, u32[]{:S(2)}) %copy-start.4) | copy-done | bytes 32792
  2.3 0.0 copy-start.7
  2.3 0.7 %copy-done.7 = bf16[2,1,64]{2,0,1:T(2,128)(2,1)S(1)} copy-done((bf16[2,1,64]{2,0,1:T(2,128)(2,1)S(1)}, bf16[2,1,64]{2,0,1:T(2,128)(2,1)}, u32[]{:S(2)}) %copy-start.7) | copy-done | bytes 280
  3.0 0.0 copy-start.5
  3.0 0.1 pack_queries.1.refs_2_
  3.1 5.1 %collective-permute-start.2 = (bf16[720,128]{1,0:T(8,128)(2,1)S(1)}, bf16[720,128]{1,0:T(8,128)(2,1)S(1)}, u32[]{:S(2)}, u32[]{:S(2)}) collective-permute-start(bf16[720,128]{1,0:T(8,128)(2,1)S(1)} %pack_queries.1.refs_2_), channel_id=1, source_target_pairs={{0,12},{4,8},{8,4},{12,0},{1,13},{5,9},{9,5},{13,1},{2,14},{6,10},... | collective-permute-start | bytes 552968 | tf_op jit(solution)/shard_map/ppermute | solution.py:394
  8.2 0.0 collective-permute-start.1
  8.2 0.6 %collective-permute-start = (bf16[720,128]{1,0:T(8,128)(2,1)S(1)}, bf16[720,128]{1,0:T(8,128)(2,1)S(1)}, u32[]{:S(2)}, u32[]{:S(2)}) collective-permute-start(bf16[720,128]{1,0:T(8,128)(2,1)S(1)} %pack_queries.1.refs_2_), channel_id=1, source_target_pairs={{0,4},{4,0},{8,12},{12,8},{1,5},{5,1},{9,13},{13,9},{2,6},{6,2},{1... | collective-permute-start | bytes 552968 | tf_op jit(solution)/shard_map/ppermute | solution.py:394
  8.8 0.0 copy-start
  8.8 2.0 %copy-done = bf16[2,1536,576]{1,2,0:T(8,128)(2,1)S(1)} copy-done((bf16[2,1536,576]{1,2,0:T(8,128)(2,1)S(1)}, bf16[2,1536,576]{1,2,0:T(8,128)(2,1)}, u32[]{:S(2)}) %copy-start) | copy-done | bytes 3538968
  10.8 0.0 copy-start.3
  10.8 0.8 %copy-done.3 = s32[2,2,2048]{2,1,0:T(2,128)S(1)} copy-done((s32[2,2,2048]{2,1,0:T(2,128)S(1)}, s32[2,2,2048]{2,1,0:T(2,128)}, u32[]{:S(2)}) %copy-start.3) | copy-done | bytes 32792
  11.6 0.0 copy-start.1
  11.6 1.1 %selection_bias.1 = (f32[2,2,1536]{2,1,0:T(2,128)S(1)}, bf16[2,576,1536]{2,1,0:T(8,128)(2,1)S(1)}) custom-call(s32[2,2,2048]{2,1,0:T(2,128)S(1)} %copy-done.3, bf16[2,576,1536]{2,1,0:T(8,128)(2,1)S(1)} %bitcast.2), custom_call_target="tpu_custom_call" | custom-call | flops 33554432 | bytes 57344 | tf_op jit(solution)/shard_map/selection_bias/pallas_call | solution.py:119
  12.7 1.1 %collective-permute-done.2.refs_5_ = bf16[720,128]{1,0:T(8,128)(2,1)S(1)} collective-permute-done((bf16[720,128]{1,0:T(8,128)(2,1)S(1)}, bf16[720,128]{1,0:T(8,128)(2,1)S(1)}, u32[]{:S(2)}, u32[]{:S(2)}) %collective-permute-start.2) | collective-permute-done | bytes 184352 | tf_op jit(solution)/shard_map/ppermute | solution.py:394
  13.8 10.0 %collective-permute-done.1.refs_4_ = bf16[720,128]{1,0:T(8,128)(2,1)S(1)} collective-permute-done((bf16[720,128]{1,0:T(8,128)(2,1)S(1)}, bf16[720,128]{1,0:T(8,128)(2,1)S(1)}, u32[]{:S(2)}, u32[]{:S(2)}) %collective-permute-start.1) | collective-permute-done | bytes 184352 | tf_op jit(solution)/shard_map/ppermute | solution.py:394
  23.8 0.0 collective-permute-done.refs_3_
  23.8 0.0 copy-done.6
  23.8 0.0 copy-done.8
  23.8 0.0 copy-done.5
  23.9 0.0 copy-done.1
  23.9 4.0 %shard_sums.1 = (f32[2,2,1536]{2,1,0:T(2,128)}, f32[128,512]{1,0:T(8,128)S(1)}, f32[16,128]{1,0:T(8,128)S(1)}, bf16[576,128]{1,0:T(8,128)(2,1)S(1)}, bf16[576,12...) custom-call(s32[2]{0:T(128)S(1)} %copy-done.6, s32[2]{0:T(128)S(1)} %copy-done.8, ...), custom_call_target="tpu_custom_call" | custom-call | tf_op jit(solution)/shard_map/shard_sums/pallas_call | solution.py:254
  27.9 0.0 collective-permute-start.4
  27.9 2.5 %collective-permute-start.5 = (bf16[576,128]{1,0:T(8,128)(2,1)S(1)}, bf16[576,128]{1,0:T(8,128)(2,1)S(1)}, u32[]{:S(2)}, u32[]{:S(2)}) collective-permute-start(bf16[576,128]{1,0:T(8,128)(2,1)S(1)} %get-tuple-element.20), channel_id=1, source_target_pairs={{0,12},{4,8},{8,4},{12,0},{1,13},{5,9},{9,5},{13,1},{2,14},{6,10},... | collective-permute-start | bytes 442376 | tf_op jit(solution)/shard_map/ppermute | solution.py:394
  30.4 1.0 %collective-permute-start.3 = (bf16[576,128]{1,0:T(8,128)(2,1)S(1)}, bf16[576,128]{1,0:T(8,128)(2,1)S(1)}, u32[]{:S(2)}, u32[]{:S(2)}) collective-permute-start(bf16[576,128]{1,0:T(8,128)(2,1)S(1)} %get-tuple-element.18.refs_3_), channel_id=1, source_target_pairs={{0,4},{4,0},{8,12},{12,8},{1,5},{5,1},{9,13},{13,9},{2,6},{6,2},{1... | collective-permute-start | bytes 442376 | tf_op jit(solution)/shard_map/ppermute | solution.py:394
  31.4 8.4 %collective-permute-done.4.refs_5_ = bf16[576,128]{1,0:T(8,128)(2,1)S(1)} collective-permute-done((bf16[576,128]{1,0:T(8,128)(2,1)S(1)}, bf16[576,128]{1,0:T(8,128)(2,1)S(1)}, u32[]{:S(2)}, u32[]{:S(2)}) %collective-permute-start.4) | collective-permute-done | bytes 147488 | tf_op jit(solution)/shard_map/ppermute | solution.py:394
  39.8 0.0 collective-permute-done.5.refs_6_
  39.8 1.3 %collective-permute-done.3.refs_4_ = bf16[576,128]{1,0:T(8,128)(2,1)S(1)} collective-permute-done((bf16[576,128]{1,0:T(8,128)(2,1)S(1)}, bf16[576,128]{1,0:T(8,128)(2,1)S(1)}, u32[]{:S(2)}, u32[]{:S(2)}) %collective-permute-start.3) | collective-permute-done | bytes 147488 | tf_op jit(solution)/shard_map/ppermute | solution.py:394
  41.0 3.2 %merge.1 = (f32[2,2]{1,0:T(2,128)}, bf16[2,1,64,512]{3,2,1,0:T(8,128)(2,1)}) custom-call(s32[2]{0:T(128)S(1)} %copy-done.6, f32[128,512]{1,0:T(8,128)S(1)} %get-tuple-element.16.refs_1_, f32[16,128]{1,0:T(8,128)S(1)} %get-tuple-element.17.refs_2_, bf16[576,128]{1,0:T(8,128)(2,1)S(1)} %get-tuple-element.18.refs_3_, ...), custom_call_target="tpu_custom_call" | custom-call | tf_op jit(solution)/shard_map/merge/pallas_call | solution.py:371
Async XLA Ops:
  0.6 23.2 %copy-start.6 = (s32[2]{0:T(128)S(1)}, s32[2]{0:T(128)}, u32[]{:S(2)}) copy-start(s32[2]{0:T(128)} %refs_0_.3) | copy-start | bytes 28
  0.6 23.2 %copy-start.8 = (s32[2]{0:T(128)S(1)}, s32[2]{0:T(128)}, u32[]{:S(2)}) copy-start(s32[2]{0:T(128)} %refs_1_.1) | copy-start | bytes 28
  0.7 0.9 %copy-start.2 = (bf16[2,1,64,576]{3,2,1,0:T(8,128)(2,1)S(1)}, bf16[2,1,64,576]{3,2,1,0:T(8,128)(2,1)}, u32[]{:S(2)}) copy-start(bf16[2,1,64,576]{3,2,1,0:T(8,128)(2,1)} %query_ref.1) | copy-start | bytes 442372
  1.6 0.8 %copy-start.4 = (bf16[2,1,64,128]{3,2,1,0:T(8,128)(2,1)S(1)}, bf16[2,1,64,128]{3,2,1,0:T(8,128)(2,1)}, u32[]{:S(2)}) copy-start(bf16[2,1,64,128]{3,2,1,0:T(8,128)(2,1)} %index_query_ref.1) | copy-start | bytes 98308
  2.3 0.7 %copy-start.7 = (bf16[2,1,64]{2,0,1:T(2,128)(2,1)S(1)}, bf16[2,1,64]{2,0,1:T(2,128)(2,1)}, u32[]{:S(2)}) copy-start(bf16[2,1,64]{2,0,1:T(2,128)(2,1)} %param.17) | copy-start | bytes 772
  3.0 20.9 %copy-start.5 = (f32[2,1536]{1,0:T(2,128)S(1)}, f32[2,1536]{1,0:T(2,128)}, u32[]{:S(2)}) copy-start(f32[2,1536]{1,0:T(2,128)} %refs_7_.1) | copy-start | bytes 36868
  3.1 10.7 %collective-permute-start.2 = (bf16[720,128]{1,0:T(8,128)(2,1)S(1)}, bf16[720,128]{1,0:T(8,128)(2,1)S(1)}, u32[]{:S(2)}, u32[]{:S(2)}) collective-permute-start(bf16[720,128]{1,0:T(8,128)(2,1)S(1)} %pack_queries.1.refs_2_), channel_id=1, source_target_pairs={{0,12},{4,8},{8,4},{12,0},{1,13},{5,9},{9,5},{13,1},{2,14},{6,10},... | collective-permute-start | bytes 552968 | tf_op jit(solution)/shard_map/ppermute | solution.py:394
  8.2 15.6 %collective-permute-start.1 = (bf16[720,128]{1,0:T(8,128)(2,1)S(1)}, bf16[720,128]{1,0:T(8,128)(2,1)S(1)}, u32[]{:S(2)}, u32[]{:S(2)}) collective-permute-start(bf16[720,128]{1,0:T(8,128)(2,1)S(1)} %pack_queries.1.refs_2_), channel_id=1, source_target_pairs={{0,8},{4,12},{8,0},{12,4},{1,9},{5,13},{9,1},{13,5},{2,10},{6,14},... | collective-permute-start | bytes 552968 | tf_op jit(solution)/shard_map/ppermute | solution.py:394
  8.2 15.6 %collective-permute-start = (bf16[720,128]{1,0:T(8,128)(2,1)S(1)}, bf16[720,128]{1,0:T(8,128)(2,1)S(1)}, u32[]{:S(2)}, u32[]{:S(2)}) collective-permute-start(bf16[720,128]{1,0:T(8,128)(2,1)S(1)} %pack_queries.1.refs_2_), channel_id=1, source_target_pairs={{0,4},{4,0},{8,12},{12,8},{1,5},{5,1},{9,13},{13,9},{2,6},{6,2},{1... | collective-permute-start | bytes 552968 | tf_op jit(solution)/shard_map/ppermute | solution.py:394
  8.8 2.0 %copy-start = (bf16[2,1536,576]{1,2,0:T(8,128)(2,1)S(1)}, bf16[2,1536,576]{1,2,0:T(8,128)(2,1)}, u32[]{:S(2)}) copy-start(bf16[2,1536,576]{1,2,0:T(8,128)(2,1)} %param.9) | copy-start | bytes 10616836
  10.8 0.8 %copy-start.3 = (s32[2,2,2048]{2,1,0:T(2,128)S(1)}, s32[2,2,2048]{2,1,0:T(2,128)}, u32[]{:S(2)}) copy-start(s32[2,2,2048]{2,1,0:T(2,128)} %selected_ref.1) | copy-start | bytes 98308
  11.6 12.3 %copy-start.1 = (bf16[2,1536,128]{2,1,0:T(8,128)(2,1)S(1)}, bf16[2,1536,128]{2,1,0:T(8,128)(2,1)}, u32[]{:S(2)}) copy-start(bf16[2,1536,128]{2,1,0:T(8,128)(2,1)} %refs_6_.1) | copy-start | bytes 2359300
  27.9 11.9 %collective-permute-start.4 = (bf16[576,128]{1,0:T(8,128)(2,1)S(1)}, bf16[576,128]{1,0:T(8,128)(2,1)S(1)}, u32[]{:S(2)}, u32[]{:S(2)}) collective-permute-start(bf16[576,128]{1,0:T(8,128)(2,1)S(1)} %get-tuple-element.19), channel_id=1, source_target_pairs={{0,8},{4,12},{8,0},{12,4},{1,9},{5,13},{9,1},{13,5},{2,10},{6,14},... | collective-permute-start | bytes 442376 | tf_op jit(solution)/shard_map/ppermute | solution.py:394
  27.9 11.9 %collective-permute-start.5 = (bf16[576,128]{1,0:T(8,128)(2,1)S(1)}, bf16[576,128]{1,0:T(8,128)(2,1)S(1)}, u32[]{:S(2)}, u32[]{:S(2)}) collective-permute-start(bf16[576,128]{1,0:T(8,128)(2,1)S(1)} %get-tuple-element.20), channel_id=1, source_target_pairs={{0,12},{4,8},{8,4},{12,0},{1,13},{5,9},{9,5},{13,1},{2,14},{6,10},... | collective-permute-start | bytes 442376 | tf_op jit(solution)/shard_map/ppermute | solution.py:394
  30.4 10.7 %collective-permute-start.3 = (bf16[576,128]{1,0:T(8,128)(2,1)S(1)}, bf16[576,128]{1,0:T(8,128)(2,1)S(1)}, u32[]{:S(2)}, u32[]{:S(2)}) collective-permute-start(bf16[576,128]{1,0:T(8,128)(2,1)S(1)} %get-tuple-element.18.refs_3_), channel_id=1, source_target_pairs={{0,4},{4,0},{8,12},{12,8},{1,5},{5,1},{9,13},{13,9},{2,6},{6,2},{1... | collective-permute-start | bytes 442376 | tf_op jit(solution)/shard_map/ppermute | solution.py:394
